TPU v7x, 32 devices: a whole 2x2x4 slice. The times are simulated.
32 devices in a mesh: ctx: 8 (over y, x, core), chan: 4 (over z).
Axes of the slice: x: 2, y: 2, z: 4, core: 2. Of those that a mesh axis runs over, the one named last changes fastest.
Arguments:
- signal: float32 [2048, 2048], P('chan', 'ctx'), may hold values from -6 to 6
- gate_in: float32 [2048, 2048], P('chan', 'ctx'), may hold values from -6 to 6
- filter_raw: float32 [2048, 2048], P('chan', 'ctx'), may hold values from -6 to 6
- short_kernel: float32 [2048, 7], P('chan'), may hold values from -2 to 2
- skip_gain: float32 [2048], P('chan'), may hold values from -4 to 4
- out_weight: float32 [2048, 2048], P(None, 'chan'), may hold values from -0.125 to 0.125
- cotangent: float32 [2048, 2048], P('chan', 'ctx'), may hold values from -6 to 6
Outputs:
- grad_gate: float32 [2048, 2048], P('chan', 'ctx')
- grad_signal: float32 [2048, 2048], P('chan', 'ctx')
- grad_filter: float32 [2048, 2048], P('chan', 'ctx')
- grad_kernel: float32 [2048, 7], P('chan')
- grad_skip: float32 [2048], P('chan')
All inputs are finite; a program needn't handle non-finite values.
Results may differ from a plain program's by a relative error of at most 0.00011.
Values sent between devices are 32-bit elements; how exact they have to be, the bound alone decides.
A program may use at most 128 MiB of HBM per device.

v0:
```python
import math

import jax
import jax.numpy as jnp
from jax import lax
from jax.sharding import PartitionSpec as P

HIGH = lax.Precision.HIGHEST


def passed_along(block, axis, distance):
    devices = range(lax.axis_size(axis))
    route = [(i - distance, i) for i in devices if i - distance in devices]
    return lax.ppermute(block, axis, route)


def angle_table(rows_len, cols_len, modulus):
    products = (
        jnp.arange(rows_len, dtype=jnp.int32)[:, None]
        * jnp.arange(cols_len, dtype=jnp.int32)[None, :]
        % modulus
    )
    return 2.0 * math.pi / modulus * products.astype(jnp.float32)


def rotate(real_part, imag_part, angles, sign):
    cosine = jnp.cos(angles)
    sine = sign * jnp.sin(angles)
    return (real_part * cosine - imag_part * sine, real_part * sine + imag_part * cosine)


def mix_last(real_part, imag_part, sign):
    span_len = real_part.shape[-1]
    angles = angle_table(span_len, span_len, span_len)
    cosine = jnp.cos(angles)
    sine = sign * jnp.sin(angles)

    def product_with(operand, table):
        return jnp.einsum("...a,ab->...b", operand, table, precision=HIGH)

    return (
        product_with(real_part, cosine) - product_with(imag_part, sine),
        product_with(real_part, sine) + product_with(imag_part, cosine),
    )


def mix_middle(real_part, imag_part, sign):
    span_len = real_part.shape[-2]
    angles = angle_table(span_len, span_len, span_len)
    cosine = jnp.cos(angles)
    sine = sign * jnp.sin(angles)

    def product_with(operand, table):
        return jnp.einsum("...ac,ab->...bc", operand, table, precision=HIGH)

    return (
        product_with(real_part, cosine) - product_with(imag_part, sine),
        product_with(real_part, sine) + product_with(imag_part, cosine),
    )


def split_len(length):
    inner_len = 128
    return (length // inner_len, inner_len)


def local_forward(real_part, imag_part):
    leading = real_part.shape[:-1]
    length = real_part.shape[-1]
    outer_len, inner_len = split_len(length)
    real_part = real_part.reshape(leading + (outer_len, inner_len))
    imag_part = imag_part.reshape(leading + (outer_len, inner_len))
    real_part, imag_part = mix_middle(real_part, imag_part, -1.0)
    real_part, imag_part = rotate(
        real_part, imag_part, angle_table(outer_len, inner_len, length), -1.0
    )
    real_part, imag_part = mix_last(real_part, imag_part, -1.0)
    return (real_part.reshape(leading + (length,)), imag_part.reshape(leading + (length,)))


def local_inverse(real_part, imag_part):
    leading = real_part.shape[:-1]
    length = real_part.shape[-1]
    outer_len, inner_len = split_len(length)
    real_part = real_part.reshape(leading + (outer_len, inner_len))
    imag_part = imag_part.reshape(leading + (outer_len, inner_len))
    real_part, imag_part = mix_last(real_part, imag_part, 1.0)
    real_part, imag_part = rotate(
        real_part, imag_part, angle_table(outer_len, inner_len, length), 1.0
    )
    real_part, imag_part = mix_middle(real_part, imag_part, 1.0)
    return (real_part.reshape(leading + (length,)), imag_part.reshape(leading + (length,)))


def block_twiddle(freqs, slice_len, modulus):
    offsets = lax.axis_index("ctx") * slice_len + jnp.arange(slice_len, dtype=jnp.int32)
    products = jnp.arange(freqs, dtype=jnp.int32)[:, None] * offsets[None, :] % modulus
    return 2.0 * math.pi / modulus * products.astype(jnp.float32)


def spectra(stacked):
    n_arrays, channels, length = stacked.shape
    devices = lax.axis_size("ctx")
    slice_len = length // devices
    freqs = 2 * devices
    modulus = freqs * length
    pieces = jnp.transpose(stacked.reshape(n_arrays, channels, devices, slice_len), (0, 2, 3, 1))
    arrived = lax.all_to_all(pieces, "ctx", split_axis=1, concat_axis=1, tiled=True)
    angles = angle_table(freqs, devices, freqs)
    real_part = jnp.einsum("qp,kprc->kqrc", jnp.cos(angles), arrived, precision=HIGH)
    imag_part = -jnp.einsum("qp,kprc->kqrc", jnp.sin(angles), arrived, precision=HIGH)
    twiddle = block_twiddle(freqs, slice_len, modulus)[:, :, None]
    real_part, imag_part = rotate(real_part, imag_part, twiddle, -1.0)
    arrived = lax.all_to_all(
        jnp.stack((real_part, imag_part)), "ctx", split_axis=2, concat_axis=3, tiled=True
    )
    arrived = jnp.moveaxis(arrived, 4, 2)
    return local_forward(arrived[0], arrived[1])


def signals(real_part, imag_part):
    real_part, imag_part = local_inverse(real_part, imag_part)
    n_arrays, channels, local_freqs, length = real_part.shape
    devices = lax.axis_size("ctx")
    slice_len = length // devices
    freqs = 2 * devices
    modulus = freqs * length
    stacked = jnp.moveaxis(jnp.stack((real_part, imag_part)), 2, 4)
    arrived = lax.all_to_all(stacked, "ctx", split_axis=3, concat_axis=2, tiled=True)
    twiddle = block_twiddle(freqs, slice_len, modulus)[:, :, None]
    real_part, imag_part = rotate(arrived[0], arrived[1], twiddle, 1.0)
    angles = angle_table(devices, freqs, freqs)
    samples = jnp.einsum("pq,kqrc->kprc", jnp.cos(angles), real_part, precision=HIGH) - jnp.einsum(
        "pq,kqrc->kprc", jnp.sin(angles), imag_part, precision=HIGH
    )
    arrived = lax.all_to_all(samples, "ctx", split_axis=1, concat_axis=2, tiled=True)
    return jnp.transpose(arrived.reshape(n_arrays, length, channels), (0, 2, 1)) / modulus


def spec_product(first, second, conjugate):
    first_real, first_imag = first
    if conjugate:
        first_imag = -first_imag
    second_real, second_imag = second
    return (
        first_real * second_real - first_imag * second_imag,
        first_real * second_imag + first_imag * second_real,
    )


def per_device(signal, gate_in, filter_raw, short_kernel, skip_gain, out_weight, cotangent):
    channels, length = signal.shape
    kernel_taps = short_kernel.shape[1]
    scale_factor = 1.0 / math.sqrt(length * lax.axis_size("ctx"))
    left_rim = passed_along(signal[:, length - (kernel_taps - 1) :], "ctx", 1)
    padded = jnp.concatenate((left_rim, signal), axis=1)
    conv_in = jnp.zeros_like(signal)
    for j in range(kernel_taps):
        conv_in = (
            conv_in
            + short_kernel[:, j : j + 1]
            * padded[:, kernel_taps - 1 - j : kernel_taps - 1 - j + length]
        )
    long_filter = filter_raw * scale_factor
    spec_real, spec_imag = spectra(jnp.stack((long_filter, conv_in)))
    filter_spec = (spec_real[0], spec_imag[0])
    value_spec = (spec_real[1], spec_imag[1])
    conv_real, conv_imag = spec_product(filter_spec, value_spec, False)
    long_conv = signals(conv_real[None], conv_imag[None])[0]
    grad_mix = jnp.dot(
        out_weight.T,
        lax.all_gather(cotangent, "chan", axis=0, tiled=True),
        precision=HIGH,
        preferred_element_type=jnp.float32,
    )
    grad_resp = grad_mix * gate_in
    grad_real, grad_imag = spectra(grad_resp[None])
    grad_spec = (grad_real[0], grad_imag[0])
    corr_spec = spec_product(filter_spec, grad_spec, True)
    filt_grad_spec = spec_product(value_spec, grad_spec, True)
    outputs = signals(
        jnp.stack((corr_spec[0], filt_grad_spec[0])), jnp.stack((corr_spec[1], filt_grad_spec[1]))
    )
    corr_part = outputs[0]
    filter_part = outputs[1]
    response = long_conv + skip_gain[:, None] * conv_in
    grad_gate = grad_mix * response
    grad_value = corr_part + skip_gain[:, None] * grad_resp
    grad_filter = filter_part * scale_factor
    right_rim = passed_along(grad_value[:, : kernel_taps - 1], "ctx", -1)
    extended = jnp.concatenate((grad_value, right_rim), axis=1)
    grad_signal = jnp.zeros_like(grad_value)
    for j in range(kernel_taps):
        grad_signal = grad_signal + short_kernel[:, j : j + 1] * extended[:, j : j + length]
    kernel_part = jnp.stack(
        [
            jnp.sum(
                grad_value * padded[:, kernel_taps - 1 - j : kernel_taps - 1 - j + length], axis=1
            )
            for j in range(kernel_taps)
        ],
        axis=1,
    )
    skip_part = jnp.sum(grad_resp * conv_in, axis=1)
    skip_sum, kernel_sum = lax.psum((skip_part, kernel_part), "ctx")
    return (grad_gate, grad_signal, grad_filter, kernel_sum * scale_factor, skip_sum * scale_factor)


def solution(mesh):
    placed = (
        P("chan", "ctx"),
        P("chan", "ctx"),
        P("chan", "ctx"),
        P("chan", None),
        P("chan"),
        P(None, "chan"),
        P("chan", "ctx"),
    )
    return jax.shard_map(
        per_device,
        mesh=mesh,
        in_specs=placed,
        out_specs=(
            P("chan", "ctx"),
            P("chan", "ctx"),
            P("chan", "ctx"),
            P("chan", None),
            P("chan"),
        ),
        check_vma=False,
    )
```

profile of v0, /device:TPU:0, one launch (start us, length us, event | category | flops | bytes accessed | tf_op | source)
XLA Modules:
  0.0 496.5 jit_solution(16550516221013616435)
XLA Ops:
  13.9 44.4 %all-gather.2.cloned.1.call-done = f32[2048,256]{1,0:T(8,128)} async-done(((f32[512,256]{1,0:T(8,128)}), f32[2048,256]{1,0:T(8,128)}) %all-gather.2.cloned.1.call-update) | async-done | bytes 2097168 | tf_op jit(solution)/shard_map/all_gather | solution.py:172
  58.2 8.1 %multiply_reduce_fusion = (f32[512]{0:T(512)S(1)}, f32[512,256]{0,1:T(8,128)}, f32[512,256]{0,1:T(8,128)S(1)}, f32[512,256]{0,1:T(8,128)}) fusion(f32[512,256]{0,1:T(8,128)S(1)} %copy.214, f32[512,256]{0,1:T(8,128)S(1)} %copy.185, f32[512,6]{0,1:T(8,128)S(1)} %collective-permute-done, f32[512]{0:T(512)S(1)} %bitcast.367, f32[512]{0:T(512)S(1)} %bitcast.369, ...), kind=kOutput, calls=%fused_computation.166 | convolution fusion | flops 3224108544 | bytes 8941568 | tf_op jit(solution)/shard_map/dot_general | solution.py:170
  66.3 3.6 all-to-all-start.4
  71.4 8.3 %all-to-all-done.4 = f32[1,8,32,512]{3,2,0,1:T(8,128)S(1)} async-done(((f32[1,8,32,512]{3,2,0,1:T(8,128)}), f32[1,8,32,512]{3,2,0,1:T(8,128)S(1)}, u32[]{:S(2)}, u32[]{:S(2)}) %all-to-all-start.4) | async-done | bytes 524320 | tf_op jit(solution)/shard_map/all_to_all | solution.py:108
  79.7 3.6 all-to-all-start
  89.2 9.4 %all-to-all-done = f32[2,8,32,512]{3,2,0,1:T(8,128)S(1)} async-done(((f32[2,8,32,512]{3,2,0,1:T(8,128)}), f32[2,8,32,512]{3,2,0,1:T(8,128)S(1)}, u32[]{:S(2)}, u32[]{:S(2)}) %all-to-all-start) | async-done | bytes 1048608 | tf_op jit(solution)/shard_map/all_to_all | solution.py:108
  98.6 3.8 all-to-all-start.5
  108.6 4.4 copy.191
  113.0 16.0 %all-to-all-done.5 = f32[2,1,16,32,512]{4,3,1,0,2:T(8,128)S(1)} async-done(((f32[2,1,16,32,512]{4,3,1,0,2:T(8,128)}), f32[2,1,16,32,512]{4,3,1,0,2:T(8,128)S(1)}, u32[]{:S(2)}, u32[]{:S(2)}) %all-to-all-start.5) | async-done | bytes 2097184 | tf_op jit(solution)/shard_map/all_to_all | solution.py:114
  129.0 4.8 all-to-all-start.1
  136.2 3.7 fusion.212
  139.9 3.8 fusion.48
  143.8 4.2 fusion.208
  148.0 6.0 %add_bitcast_fusion.2 = (f32[512,2,2,128]{3,2,1,0:T(2,128)S(1)}, f32[512,2,2,128]{3,2,1,0:T(2,128)S(1)}) fusion(f32[2,1,512,2,128]{4,0,3,2,1:T(2,128)S(1)} %fusion.48, f32[2,128]{1,0:T(2,128)S(1)} %get-tuple-element.83, f32[2,128]{1,0:T(2,128)S(1)} %get-tuple-element.84, f32[2,512,2,128]{3,0,2,1:T(2,128)S(1)} %fusion.208, f32[512,2,2,128]{3,2,1,0:T(2,128)} %copy-done.15), kind=kOutput, calls=%fused_computation.105 | convolution fusion | flops 8126520 | bytes 5244928 | tf_op jit(solution)/shard_map/...ac,ab->...bc/dot_general | solution.py:54
  159.8 23.2 %all-to-all-done.1 = f32[2,2,16,32,512]{4,3,1,0,2:T(8,128)} async-done(((f32[2,2,16,32,512]{4,3,1,0,2:T(8,128)}), f32[2,2,16,32,512]{4,3,1,0,2:T(8,128)}, u32[]{:S(2)}, u32[]{:S(2)}) %all-to-all-start.1) | async-done | bytes 4194336 | tf_op jit(solution)/shard_map/all_to_all | solution.py:114
  188.4 3.1 copy.258
  191.5 8.8 %fusion.221 = f32[2,2,512,2,128]{4,0,3,2,1:T(2,128)} fusion(f32[2,512,2,2,128]{4,3,2,1,0:T(2,128)S(1)} %copy.258), kind=kOutput, calls=%fused_computation.285 | convolution fusion | flops 12582968 | bytes 4194304 | tf_op jit(solution)/shard_map/...ac,ab->...bc/dot_general | solution.py:54
  200.3 8.7 %fusion.223 = f32[2,2,512,2,128]{4,0,3,2,1:T(2,128)} fusion(f32[2,512,2,2,128]{4,3,2,1,0:T(2,128)S(1)} %copy.258), kind=kOutput, calls=%fused_computation.287 | convolution fusion | flops 12582972 | bytes 4194304 | tf_op jit(solution)/shard_map/...ac,ab->...bc/dot_general | solution.py:54
  212.1 9.6 %convolution_subtract_fusion = f32[2,2,512,2,128]{4,0,3,2,1:T(2,128)S(1)} fusion(f32[2,2,512,2,128]{4,0,3,2,1:T(2,128)} %fusion.221, f32[2,512,2,2,128]{4,3,2,1,0:T(2,128)S(1)} %copy.259), kind=kOutput, calls=%fused_computation.43 | convolution fusion | flops 13107260 | bytes 6291456 | tf_op jit(solution)/shard_map/...ac,ab->...bc/dot_general | solution.py:54
  221.7 9.9 %subtract_bitcast_fusion.1 = (f32[2,512,2,2,128]{4,3,2,1,0:T(2,128)S(1)}, f32[2,512,2,2,128]{4,3,2,1,0:T(2,128)S(1)}) fusion(f32[2,2,512,2,128]{4,0,3,2,1:T(2,128)S(1)} %convolution_subtract_fusion, f32[2,128]{1,0:T(2,128)S(1)} %get-tuple-element.83, f32[2,128]{1,0:T(2,128)S(1)} %get-tuple-element.84, f32[2,2,512,2,128]{4,0,3,2,1:T(2,128)S(1)} %copy-done.12, ...), kind=kOutput, calls=%fused_computation.27 | convolution fusion | flops 16252984 | bytes 10487808 | tf_op jit(solution)/shard_map/...ac,ab->...bc/dot_general | solution.py:54
  247.1 4.9 fusion.81
  252.1 5.9 %fusion.79 = f32[2,512,2,128]{3,0,2,1:T(2,128)} fusion(f32[512,2,2,128]{3,0,2,1:T(8,128)S(1)} %get-tuple-element.66), kind=kOutput, calls=%fused_computation.127 | convolution fusion | flops 6291512 | bytes 2097152 | tf_op jit(solution)/shard_map/...ac,ab->...bc/dot_general | solution.py:54
  258.0 3.4 fusion.20
  261.5 3.4 fusion.21
  264.9 6.0 %fusion.50 = f32[1,512,2,2,128]{4,3,2,1,0:T(2,128)} fusion(f32[2,512,2,128]{3,0,2,1:T(2,128)S(1)} %fusion.81, f32[512,2,2,128]{3,0,2,1:T(8,128)S(1)} %get-tuple-element.65), kind=kOutput, calls=%fused_computation.80 | convolution fusion | flops 6553656 | bytes 3145728 | tf_op jit(solution)/shard_map/...ac,ab->...bc/dot_general | solution.py:54
  273.3 7.0 %fusion.49 = f32[1,512,2,2,128]{4,3,2,1,0:T(2,128)} fusion(f32[2,512,2,128]{3,0,2,1:T(2,128)} %fusion.79, f32[512,2,2,128]{3,0,2,1:T(8,128)} %copy-done.14), kind=kOutput, calls=%fused_computation.78 | convolution fusion | flops 6553656 | bytes 3145728 | tf_op jit(solution)/shard_map/...ac,ab->...bc/dot_general | solution.py:54
  280.4 4.0 copy.261
  284.4 3.5 maximum_bitcast_fusion.1
  287.9 4.4 all-to-all-start.2
  292.3 3.8 fusion.24
  296.1 3.7 multiply_add_fusion
  299.8 8.1 %fusion.36 = f32[2,2,512,2,128]{4,0,3,2,1:T(2,128)S(1)} fusion(f32[2,512,2,2,128]{4,1,3,2,0:T(8,128)S(1)} %get-tuple-element.50), kind=kOutput, calls=%fused_computation.50 | convolution fusion | flops 12582968 | bytes 4194304 | tf_op jit(solution)/shard_map/...ac,ab->...bc/dot_general | solution.py:54
  307.9 9.8 %subtract_bitcast_fusion = f32[2,512,2,2,128]{4,3,2,1,0:T(2,128)} fusion(f32[2,2,512,2,128]{4,0,3,2,1:T(2,128)S(1)} %fusion.36, f32[2,512,2,2,128]{4,1,3,2,0:T(8,128)S(1)} %get-tuple-element.49), kind=kOutput, calls=%fused_computation.23 | convolution fusion | flops 13107256 | bytes 6291456 | tf_op jit(solution)/shard_map/...ac,ab->...bc/dot_general | solution.py:54
  317.7 6.1 %copy.264 = f32[2,512,2,2,128]{1,2,0,4,3:T(2,128)} copy(f32[2,512,2,2,128]{4,3,2,1,0:T(2,128)} %subtract_bitcast_fusion) | data formatting | bytes 4194304 | tf_op jit(solution)/shard_map/stack;reshape | solution.py:128
  323.8 8.1 %fusion.34 = f32[2,2,512,2,128]{4,0,3,2,1:T(2,128)S(1)} fusion(f32[2,512,2,2,128]{4,1,3,2,0:T(8,128)S(1)} %get-tuple-element.50), kind=kOutput, calls=%fused_computation.48 | convolution fusion | flops 12582968 | bytes 4194304 | tf_op jit(solution)/shard_map/...ac,ab->...bc/dot_general | solution.py:54
  331.9 9.9 %add_bitcast_fusion = f32[2,512,2,2,128]{4,3,2,1,0:T(2,128)} fusion(f32[2,2,512,2,128]{4,0,3,2,1:T(2,128)S(1)} %fusion.34, f32[2,512,2,2,128]{4,1,3,2,0:T(8,128)S(1)} %copy-done.11), kind=kOutput, calls=%fused_computation.22 | convolution fusion | flops 13107256 | bytes 6291456 | tf_op jit(solution)/shard_map/...ac,ab->...bc/dot_general | solution.py:54
  341.8 6.3 %copy.265 = f32[2,512,2,2,128]{1,2,0,4,3:T(2,128)} copy(f32[2,512,2,2,128]{4,3,2,1,0:T(2,128)} %add_bitcast_fusion) | data formatting | bytes 4194304 | tf_op jit(solution)/shard_map/stack;reshape | solution.py:128
  348.0 5.7 %maximum_bitcast_fusion = f32[2,2,2,256,512]{4,2,1,0,3:T(2,128)} fusion(f32[1,2,512,2,256]{2,3,1,0,4:T(2,128)} %bitcast.348, f32[1,2,512,2,256]{2,3,1,0,4:T(2,128)S(1)} %bitcast.345), kind=kLoop, calls=%fused_computation.1 | loop fusion | flops 1048576 | bytes 8388608 | tf_op jit(solution)/shard_map/transpose | solution.py:128
  353.8 4.6 all-to-all-start.6
  365.3 42.2 %all-to-all-done.6 = f32[2,2,2,256,512]{4,2,1,0,3:T(2,128)} async-done(((f32[2,2,2,256,512]{4,2,1,0,3:T(2,128)}), f32[2,2,2,256,512]{4,2,1,0,3:T(2,128)}, u32[]{:S(2)}, u32[]{:S(2)}) %all-to-all-start.6) | async-done | bytes 4194336 | tf_op jit(solution)/shard_map/all_to_all | solution.py:129
  407.5 3.7 all-to-all-start.3
  411.2 4.6 copy.232
  423.5 4.5 copy.234
  428.0 3.6 squeeze.27
  431.6 3.3 fusion.4
  438.2 4.2 all-to-all-start.7
  442.4 15.4 %all-to-all-done.7 = f32[2,8,32,512]{3,2,0,1:T(8,128)S(1)} async-done(((f32[2,8,32,512]{3,2,0,1:T(8,128)}), f32[2,8,32,512]{3,2,0,1:T(8,128)S(1)}, u32[]{:S(2)}, u32[]{:S(2)}) %all-to-all-start.7) | async-done | bytes 1048608 | tf_op jit(solution)/shard_map/all_to_all | solution.py:136
  460.9 22.3 %all-reduce = (f32[512,7]{0,1:T(8,128)S(1)}, f32[512]{0:T(512)S(1)}) all-reduce(f32[512,7]{0,1:T(8,128)S(1)} %stack.87, f32[512]{0:T(512)S(1)} %get-tuple-element.39), channel_id=1, replica_groups=mesh['ctx'=8,'chan'=4] {'ctx'}, use_global_device_ids=true, to_apply=%region_7.8 | all-reduce | flops 4096 | bytes 32768 | tf_op jit(solution)/shard_map/psum | solution.py:205
  (112 shorter events, 81.4 us)
Async XLA Ops:
  7.2 51.1 %all-gather.2.cloned.1.call-start = ((), (), s32[]{:S(2)}) async-start(), calls=%async_computation.8 | async-start | bytes 2621440 | tf_op jit(solution)/shard_map/all_gather | solution.py:172
  9.1 57.2 %copy-start.4 = (f32[512,256]{0,1:T(8,128)}, f32[512,256]{0,1:T(8,128)S(1)}, u32[]{:S(2)}) copy-start(f32[512,256]{0,1:T(8,128)S(1)} %copy.185) | copy-start | bytes 1572868
  9.2 4.7 collective-permute-start
  58.2 11.7 %copy-start.16 = (f32[512,256]{1,0:T(8,128)S(1)}, f32[512,256]{1,0:T(8,128)}, u32[]{:S(2)}) copy-start(f32[512,256]{1,0:T(8,128)} %param.9) | copy-start | bytes 1572868
  66.3 4.0 copy-start.6
  66.3 13.4 %all-to-all-start.4 = ((f32[1,8,32,512]{3,2,0,1:T(8,128)}), f32[1,8,32,512]{3,2,0,1:T(8,128)S(1)}, u32[]{:S(2)}, u32[]{:S(2)}) async-start(f32[1,8,32,512]{3,2,0,1:T(8,128)} %bitcast.75), calls=%async_computation.4 | async-start | bytes 1048576 | tf_op jit(solution)/shard_map/all_to_all | solution.py:108
  79.7 18.9 %all-to-all-start = ((f32[2,8,32,512]{3,2,0,1:T(8,128)}), f32[2,8,32,512]{3,2,0,1:T(8,128)S(1)}, u32[]{:S(2)}, u32[]{:S(2)}) async-start(f32[2,8,32,512]{3,2,0,1:T(8,128)} %copy.188), calls=%async_computation | async-start | bytes 2097152 | tf_op jit(solution)/shard_map/all_to_all | solution.py:108
  98.6 30.4 %all-to-all-start.5 = ((f32[2,1,16,32,512]{4,3,1,0,2:T(8,128)}), f32[2,1,16,32,512]{4,3,1,0,2:T(8,128)S(1)}, u32[]{:S(2)}, u32[]{:S(2)}) async-start(f32[2,1,16,32,512]{4,3,1,0,2:T(8,128)} %copy.217), calls=%async_computation.5 | async-start | bytes 4194304 | tf_op jit(solution)/shard_map/all_to_all | solution.py:114
  129.0 54.0 %all-to-all-start.1 = ((f32[2,2,16,32,512]{4,3,1,0,2:T(8,128)}), f32[2,2,16,32,512]{4,3,1,0,2:T(8,128)}, u32[]{:S(2)}, u32[]{:S(2)}) async-start(f32[2,2,16,32,512]{4,3,1,0,2:T(8,128)} %copy.191), calls=%async_computation.1 | async-start | bytes 8388608 | tf_op jit(solution)/shard_map/all_to_all | solution.py:114
  136.2 7.6 %copy-start.15 = (f32[512,2,2,128]{3,2,1,0:T(2,128)}, f32[512,2,2,128]{3,2,1,0:T(2,128)S(1)}, u32[]{:S(2)}) copy-start(f32[512,2,2,128]{3,2,1,0:T(2,128)S(1)} %copy.263) | copy-start | bytes 3145732
  212.1 9.6 %copy-start.12 = (f32[2,2,512,2,128]{4,0,3,2,1:T(2,128)S(1)}, f32[2,2,512,2,128]{4,0,3,2,1:T(2,128)}, u32[]{:S(2)}) copy-start(f32[2,2,512,2,128]{4,0,3,2,1:T(2,128)} %fusion.223) | copy-start | bytes 6291460
  237.9 2.1 copy-start.8
  237.9 2.1 copy-start.9
  241.8 50.4 %copy-start.1 = (f32[1,512,2,2,128]{4,1,3,2,0:T(8,128)}, f32[1,512,2,2,128]{4,1,3,2,0:T(8,128)S(1)}, u32[]{:S(2)}) copy-start(f32[1,512,2,2,128]{4,1,3,2,0:T(8,128)S(1)} %get-tuple-element.46) | copy-start | bytes 3145732
  247.1 17.7 %copy-start.14 = (f32[512,2,2,128]{3,0,2,1:T(8,128)}, f32[512,2,2,128]{3,0,2,1:T(8,128)S(1)}, u32[]{:S(2)}) copy-start(f32[512,2,2,128]{3,0,2,1:T(8,128)S(1)} %get-tuple-element.65) | copy-start | bytes 3145732
  287.9 65.9 %all-to-all-start.2 = ((f32[2,1,2,256,512]{4,2,0,1,3:T(2,128)}), f32[2,1,2,256,512]{4,2,0,1,3:T(2,128)}, u32[]{:S(2)}, u32[]{:S(2)}) async-start(f32[2,1,2,256,512]{4,2,0,1,3:T(2,128)} %maximum_bitcast_fusion.1), calls=%async_computation.2 | async-start | bytes 4194304 | tf_op jit(solution)/shard_map/all_to_all | solution.py:129
  292.2 3.9 copy-start.2
  299.8 8.1 %copy-start.10 = (f32[2,512,2,2,128]{4,1,3,2,0:T(8,128)}, f32[2,512,2,2,128]{4,1,3,2,0:T(8,128)S(1)}, u32[]{:S(2)}) copy-start(f32[2,512,2,2,128]{4,1,3,2,0:T(8,128)S(1)} %get-tuple-element.49) | copy-start | bytes 6291460
  323.8 8.1 %copy-start.11 = (f32[2,512,2,2,128]{4,1,3,2,0:T(8,128)S(1)}, f32[2,512,2,2,128]{4,1,3,2,0:T(8,128)}, u32[]{:S(2)}) copy-start(f32[2,512,2,2,128]{4,1,3,2,0:T(8,128)} %copy-done.10) | copy-start | bytes 6291460
  341.8 6.3 %copy-start.3 = (f32[2,512,2,2,128]{1,2,0,4,3:T(2,128)S(1)}, f32[2,512,2,2,128]{1,2,0,4,3:T(2,128)}, u32[]{:S(2)}) copy-start(f32[2,512,2,2,128]{1,2,0,4,3:T(2,128)} %copy.264) | copy-start | bytes 6291460
  353.8 53.7 %all-to-all-start.6 = ((f32[2,2,2,256,512]{4,2,1,0,3:T(2,128)}), f32[2,2,2,256,512]{4,2,1,0,3:T(2,128)}, u32[]{:S(2)}, u32[]{:S(2)}) async-start(f32[2,2,2,256,512]{4,2,1,0,3:T(2,128)} %maximum_bitcast_fusion), calls=%async_computation.6 | async-start | bytes 8388608 | tf_op jit(solution)/shard_map/all_to_all | solution.py:129
  407.5 30.7 %all-to-all-start.3 = ((f32[1,8,32,512]{3,2,0,1:T(8,128)}), f32[1,8,32,512]{3,2,0,1:T(8,128)S(1)}, u32[]{:S(2)}, u32[]{:S(2)}) async-start(f32[1,8,32,512]{3,2,0,1:T(8,128)} %copy.213), calls=%async_computation.3 | async-start | bytes 1048576 | tf_op jit(solution)/shard_map/all_to_all | solution.py:136
  431.6 3.3 copy-start
  438.2 19.6 %all-to-all-start.7 = ((f32[2,8,32,512]{3,2,0,1:T(8,128)}), f32[2,8,32,512]{3,2,0,1:T(8,128)S(1)}, u32[]{:S(2)}, u32[]{:S(2)}) async-start(f32[2,8,32,512]{3,2,0,1:T(8,128)} %copy.235), calls=%async_computation.7 | async-start | bytes 2097152 | tf_op jit(solution)/shard_map/all_to_all | solution.py:136
  457.9 1.0 copy-start.5
  457.9 1.2 copy-start.7
  457.9 1.3 copy-start.13
  457.9 1.3 copy-start.17
  483.9 3.9 collective-permute-start.1
Sparse Core Ops, SparseCore 0:
  9.6 48.6 all-gather.1
where the time goes:
time: 506 us; the launch traced here: 497 us
  matrix products  174 us (34%)
  waiting for transfers between devices  159 us (31%)
  local copies, waits for them, and re-layouts  74.8 us (15%)
  starting transfers between devices  36.4 us (7%)
  blocking collectives  22.3 us (4%)
  between operations  15.3 us (3%)
  other arithmetic  14.5 us (3%)
    dot_general x16, matrix products, product_with(): return jnp.einsum('...ac,ab->...bc', operand, table, precision=HIGH)  114 us
    all_gather x1, waiting for transfers between devices, per_device(): lax.all_gather(cotangent, 'chan', axis=0, tiled=True)  44.4 us
    all_to_all x2, waiting for transfers between devices, signals(): lax.all_to_all(stacked, 'ctx', split_axis=3, concat_axis=2, tiled=True)  42.2 us
    all_to_all x2, waiting for transfers between devices, spectra(): lax.all_to_all(jnp.stack((real_part, imag_part)), 'ctx', split_axis=2, co...  39.2 us
    dot_general x16, matrix products, product_with(): return jnp.einsum('...a,ab->...b', operand, table, precision=HIGH)  35.5 us
    psum x1, blocking collectives, per_device(): skip_sum, kernel_sum = lax.psum((skip_part, kernel_part), 'ctx')  22.3 us
    another operation x4, local copies, waits for them, and re-layouts, signals(): stacked = jnp.moveaxis(jnp.stack((real_part, imag_part)), 2, 4)  18.9 us
    all_to_all x2, waiting for transfers between devices, spectra(): lax.all_to_all(pieces, 'ctx', split_axis=1, concat_axis=1, tiled=True)  17.7 us
  transfers between devices with their start and end apart: 11, of which 7 were waited for; matrix products, arithmetic and copies ran while one was open for 29% of the time, Pallas kernels for 0%

commit v1 on v0

v1 whole, which is shorter than its diff:
```python
import functools
import math

import jax
import jax.numpy as jnp
import numpy as np
from jax import lax
from jax.experimental import pallas as pl
from jax.experimental.pallas import tpu as pltpu
from jax.sharding import PartitionSpec as P

MESH = pl.DeviceIdType.MESH
F32 = jnp.float32
BF16 = jnp.bfloat16
SIG, FIL, RESP, GSIG, GFIL, SMALL, GRAD = range(7)


def split_bf16(value):
    high = value.astype(BF16)
    return high, (value - high.astype(F32)).astype(BF16)


def tables(blocks, length, scale):
    total = 2 * blocks * length
    turn = np.arange(blocks + 1)[:, None] * np.arange(length)[None, :] % total
    angle = 2.0 * np.pi / total * turn
    weight = np.full((blocks + 1, 1), 2.0)
    weight[0] = weight[blocks] = 1.0
    weight = weight * (scale / total)
    twiddle = np.stack(
        (np.cos(angle), np.sin(angle), weight * np.cos(angle), weight * np.sin(angle))
    ).astype(np.float32)
    turn = np.arange(length)[:, None] * np.arange(length)[None, :] % length
    angle = 2.0 * np.pi / length * turn
    cosine, sine = np.cos(angle), np.sin(angle)
    matrix = np.block([[cosine, -sine], [sine, cosine]]).astype(np.float32)
    high = matrix.astype(jnp.bfloat16)
    low = (matrix - high.astype(np.float32)).astype(jnp.bfloat16)
    return twiddle, high, low


def weighted_sum(terms):
    total = None
    for factor, value in terms:
        if abs(factor) < 1e-12:
            continue
        if abs(factor - 1.0) < 1e-12:
            part = value
        elif abs(factor + 1.0) < 1e-12:
            part = -value
        else:
            part = np.float32(factor) * value
        total = part if total is None else total + part
    return total


def forward_blocks(parts, twiddle, store):
    blocks = len(parts)

    def put(q, real, imag):
        cosine, sine = twiddle[0, q : q + 1, :], twiddle[1, q : q + 1, :]
        if imag is None:
            store(q, real * cosine, -real * sine)
        else:
            store(q, real * cosine + imag * sine, imag * cosine - real * sine)

    for q in range(blocks // 2 + 1):
        def gather(first, trig, sign):
            return weighted_sum(
                [(sign * trig(math.pi * a * q / blocks), parts[a]) for a in range(first, blocks, 2)]
            )

        even_re, even_im = gather(0, math.cos, 1.0), gather(0, math.sin, -1.0)
        odd_re, odd_im = gather(1, math.cos, 1.0), gather(1, math.sin, -1.0)

        def add(a, b, sign_a, sign_b):
            return weighted_sum([(s, v) for s, v in ((sign_a, a), (sign_b, b)) if v is not None])

        put(q, add(even_re, odd_re, 1.0, 1.0), add(even_im, odd_im, 1.0, 1.0))
        if q != blocks - q:
            put(blocks - q, add(even_re, odd_re, 1.0, -1.0), add(even_im, odd_im, -1.0, 1.0))


def inverse_blocks(blocks, length, twiddle, load):
    def real_imag(q):
        pair = load(q)
        real, minus = pair[:, :length], pair[:, length:]
        cosine, sine = twiddle[2, q : q + 1, :], twiddle[3, q : q + 1, :]
        return real * cosine + minus * sine, real * sine - minus * cosine

    first, last = real_imag(0)[0], real_imag(blocks)[0]
    half_re, half_im = real_imag(blocks // 2)
    pairs = []
    for q in range(1, blocks // 2):
        (re_a, im_a), (re_b, im_b) = real_imag(q), real_imag(blocks - q)
        pairs.append((re_a + re_b, im_a - im_b, re_a - re_b, im_a + im_b))
    result = []
    for a in range(blocks):
        odd = a % 2
        terms = [(1.0, first - last if odd else first + last)]
        terms.append((math.cos(math.pi * a / 2), half_re))
        terms.append((-math.sin(math.pi * a / 2), half_im))
        for q in range(1, blocks // 2):
            angle = math.pi * a * q / blocks
            terms.append((math.cos(angle), pairs[q - 1][2 * odd]))
            terms.append((-math.sin(angle), pairs[q - 1][2 * odd + 1]))
        result.append(weighted_sum(terms))
    return result


def kernel(
    dims,
    sig_in, gate_in, fil_in, taps_ref, w_in, cot_in, twiddle, high_ref, low_ref,
    gate_out, gsig_out, gfil_out, small_out,
    w_buf, wt_hi, wt_lo, cot_all, mix, gate_buf, sig_buf, fil_buf, conv_buf,
    resp_send, resp_buf, grad_send, grad_buf, gsig_send, gfil_send, small_buf, small_send,
    stage, fil_spec, val_spec, grad_spec, work,
    up_sem, down_sem, line_sem, send_sem, recv_sem, local_sem, load_sem,
):
    devices, groups, rows, rows_pad, length, taps, halves, scale = dims
    me, chan = lax.axis_index("ctx"), lax.axis_index("chan")
    half_len = length // halves
    group_rows = min(8, rows)
    row_steps = rows // group_rows
    classes = devices + 1
    chunk = 3 if classes % 3 == 0 else 1

    w_copy = pltpu.make_async_copy(w_in, w_buf, load_sem.at[0])
    gate_copy = pltpu.make_async_copy(gate_in, gate_buf, load_sem.at[1])
    cot_copy = pltpu.make_async_copy(cot_in, cot_all.at[chan], load_sem.at[2])
    w_copy.start()
    cot_copy.start()
    gate_copy.start()

    barrier = pltpu.get_barrier_semaphore()

    @pl.loop(1, devices)
    def _(k):
        pl.semaphore_signal(
            barrier, inc=1, device_id={"ctx": lax.rem(me + k, devices)}, device_id_type=MESH
        )

    @pl.loop(1, groups)
    def _(k):
        pl.semaphore_signal(
            barrier, inc=1, device_id={"chan": lax.rem(chan + k, groups)}, device_id_type=MESH
        )

    pl.semaphore_wait(barrier, devices + groups - 2)

    def lanes(h):
        return pl.ds(h * half_len, half_len)

    def hop(step, h, up):
        block = chan - step if up else chan + step
        source = cot_in if step == 0 else cot_all.at[block]
        sems = up_sem if up else down_sem
        return pltpu.make_async_remote_copy(
            src_ref=source.at[:, lanes(h)],
            dst_ref=cot_all.at[block, :, lanes(h)],
            send_sem=sems.at[h, step],
            recv_sem=line_sem.at[h, block],
            device_id={"chan": chan + 1 if up else chan - 1},
            device_id_type=MESH,
        )

    def sends(step, up):
        if up:
            return jnp.logical_and(chan - step >= 0, chan + 1 < groups)
        return jnp.logical_and(chan + step < groups, chan >= 1)

    def arrives(step, up):
        return chan - step >= 0 if up else chan + step < groups

    def line_start(step, h):
        for up in (True, False):
            @pl.when(sends(step, up))
            def _():
                hop(step, h, up).start()

    def line_arrive(step, h):
        for up in (True, False):
            @pl.when(arrives(step, up))
            def _():
                block = chan - step if up else chan + step
                slot = cot_all.at[block, :, lanes(h)]
                pltpu.make_async_remote_copy(
                    src_ref=slot,
                    dst_ref=slot,
                    send_sem=up_sem.at[h, step],
                    recv_sem=line_sem.at[h, block],
                    device_id={"chan": chan - 1 if up else chan + 1},
                    device_id_type=MESH,
                ).wait_recv()

                @pl.when(sends(step, up))
                def _():
                    hop(step, h, up).start()

    def all_to_all(index, source, target):
        def piece(k):
            peer = lax.rem(me + k, devices)
            return pltpu.make_async_remote_copy(
                src_ref=source(peer),
                dst_ref=target(me),
                send_sem=send_sem.at[index, k],
                recv_sem=recv_sem.at[index, k],
                device_id={"ctx": peer},
                device_id_type=MESH,
            )

        own = pltpu.make_async_copy(source(me), target(me), local_sem.at[index])

        def start():
            @pl.loop(1, devices)
            def _(k):
                piece(k).start()

            own.start()

        def arrive():
            @pl.loop(1, devices)
            def _(k):
                piece(k).wait_recv()

            own.wait()

        def sent():
            @pl.loop(1, devices)
            def _(k):
                piece(k).wait_send()

        return start, arrive, sent

    sig_start, sig_arrive, sig_sent = all_to_all(SIG, lambda p: sig_in.at[p], lambda p: sig_buf.at[p])
    fil_start, fil_arrive, fil_sent = all_to_all(FIL, lambda p: fil_in.at[p], lambda p: fil_buf.at[p])
    resp_start, resp_arrive, resp_sent = all_to_all(
        RESP, lambda p: resp_send.at[p], lambda p: resp_buf.at[p]
    )
    gsig_start, gsig_arrive, gsig_sent = all_to_all(
        GSIG, lambda p: gsig_send.at[p], lambda p: gsig_out.at[p]
    )
    gfil_start, gfil_arrive, gfil_sent = all_to_all(
        GFIL, lambda p: gfil_send.at[p], lambda p: gfil_out.at[p]
    )
    small_start, small_arrive, small_sent = all_to_all(
        SMALL, lambda p: small_send, lambda p: small_out.at[p]
    )
    grad_moves = [
        all_to_all(
            GRAD + h,
            lambda p, h=h: grad_send.at[p, :, lanes(h)],
            lambda p, h=h: grad_buf.at[p, :, lanes(h)],
        )
        for h in range(halves)
    ]

    for h in range(halves):
        line_start(0, h)
    sig_start()
    fil_start()

    def dft(read, target):
        @pl.loop(0, classes // chunk)
        def _(i):
            at = pl.ds(i * chunk, chunk)
            high, low = split_bf16(read(at))
            result = jnp.dot(high, low_ref[...], preferred_element_type=F32)
            result = result + jnp.dot(low, high_ref[...], preferred_element_type=F32)
            result = result + jnp.dot(high, high_ref[...], preferred_element_type=F32)
            target[at] = result.reshape(chunk, rows_pad, 2 * length)

    def plain(at):
        return stage[at].reshape(chunk * rows_pad, 2 * length)

    def product(first, second, conjugate):
        def read(at):
            a_re, a_im = first[at, :, :length], first[at, :, length:]
            b_re, b_im = second[at, :, :length], second[at, :, length:]
            if conjugate:
                real, minus = a_re * b_re + a_im * b_im, a_im * b_re - a_re * b_im
            else:
                real, minus = a_re * b_re - a_im * b_im, -(a_re * b_im + a_im * b_re)
            return jnp.concatenate((real, minus), axis=2).reshape(chunk * rows_pad, 2 * length)

        return read

    def over_rows(body):
        @pl.loop(0, row_steps)
        def _(r):
            body(pl.ds(pl.multiple_of(r * group_rows, group_rows), group_rows))

    def stage_store(at):
        def store(q, real, imag):
            stage[q, at, :length] = real
            stage[q, at, length:] = imag

        return store

    def tap_rows(at):
        return taps_ref[me, at, :]

    def delayed(parts, a, j):
        if j == 0:
            return parts[a]
        before = jnp.zeros_like(parts[a][:, :128]) if a == 0 else parts[a - 1][:, length - 128 :]
        joined = jnp.concatenate((before, parts[a]), axis=1)
        return pltpu.roll(joined, j, 1)[:, 128:]

    def advanced(parts, a, j):
        if j == 0:
            return parts[a]
        after = jnp.zeros_like(parts[a][:, :128]) if a == devices - 1 else parts[a + 1][:, :128]
        joined = jnp.concatenate((parts[a], after), axis=1)
        return pltpu.roll(joined, length + 128 - j, 1)[:, :length]

    w_copy.wait()

    @pl.loop(0, groups)
    def _(g):
        turned = w_buf[g].T
        high, low = split_bf16(turned)
        wt_hi[g] = high
        wt_lo[g] = low

    cot_copy.wait()

    def mix_add(block, h, first):
        high, low = split_bf16(cot_all[block, :, h * half_len : (h + 1) * half_len])
        result = jnp.dot(wt_lo[block], high, preferred_element_type=F32)
        result = result + jnp.dot(wt_hi[block], low, preferred_element_type=F32)
        result = result + jnp.dot(wt_hi[block], high, preferred_element_type=F32)
        at = (slice(None), slice(h * half_len, (h + 1) * half_len))
        mix[at] = result if first else mix[at] + result

    def mix_step(step, h):
        for up in (True, False):
            @pl.when(arrives(step, up))
            def _():
                mix_add(chan - step if up else chan + step, h, False)

    for h in range(halves):
        mix_add(chan, h, True)

    sig_arrive()

    def conv_rows(at):
        tap = tap_rows(at)
        parts = [sig_buf[a, at, :] for a in range(devices)]
        conv = []
        for a in range(devices):
            total = tap[:, :1] * parts[a]
            for j in range(1, taps):
                total = total + tap[:, j : j + 1] * delayed(parts, a, j)
            conv_buf[a, at, :] = total
            conv.append(total)
        forward_blocks(conv, twiddle, stage_store(at))

    over_rows(conv_rows)
    dft(plain, val_spec)

    for h in range(halves):
        if groups > 1:
            line_arrive(1, h)

    fil_arrive()
    over_rows(
        lambda at: forward_blocks(
            [fil_buf[a, at, :] for a in range(devices)], twiddle, stage_store(at)
        )
    )
    dft(plain, fil_spec)
    if groups > 1:
        for h in range(halves):
            mix_step(1, h)
    dft(product(fil_spec, val_spec, False), work)

    def resp_rows(at):
        skip = tap_rows(at)[:, taps : taps + 1]
        conv = inverse_blocks(devices, length, twiddle, lambda q: work[q, at, :])
        for a in range(devices):
            resp_send[a, at, :] = conv[a] + skip * conv_buf[a, at, :]

    over_rows(resp_rows)
    resp_start()

    for step in range(2, groups - 1):
        for h in range(halves):
            line_arrive(step, h)
            mix_step(step, h)
    gate_copy.wait()
    for h in range(halves):
        if groups > 2:
            line_arrive(groups - 1, h)
            mix_step(groups - 1, h)
        here = slice(h * half_len, (h + 1) * half_len)
        for d in range(devices):
            grad_send[d, :, here] = mix[d * rows : (d + 1) * rows, here] * gate_buf[d, :, here]
        grad_moves[h][0]()

    resp_arrive()
    for d in range(devices):
        gate_out[d] = mix[d * rows : (d + 1) * rows, :] * resp_buf[d]

    for _, grad_arrive, _ in grad_moves:
        grad_arrive()

    over_rows(
        lambda at: forward_blocks(
            [grad_buf[a, at, :] for a in range(devices)], twiddle, stage_store(at)
        )
    )
    dft(plain, grad_spec)
    dft(product(val_spec, grad_spec, True), work)

    def filter_rows(at):
        parts = inverse_blocks(devices, length, twiddle, lambda q: work[q, at, :])
        for a in range(devices):
            gfil_send[a, at, :] = parts[a]

    over_rows(filter_rows)
    gfil_start()
    dft(product(fil_spec, grad_spec, True), work)

    def value_rows(at):
        tap = tap_rows(at)
        skip = tap[:, taps : taps + 1]
        value = inverse_blocks(devices, length, twiddle, lambda q: work[q, at, :])
        grad = [grad_buf[a, at, :] for a in range(devices)]
        value = [value[a] + skip * grad[a] for a in range(devices)]
        for a in range(devices):
            total = tap[:, :1] * value[a]
            for j in range(1, taps):
                total = total + tap[:, j : j + 1] * advanced(value, a, j)
            gsig_send[a, at, :] = total
        signal = [sig_buf[a, at, :] for a in range(devices)]
        lane = lax.broadcasted_iota(jnp.int32, (group_rows, 128), 1)
        sums = jnp.zeros((group_rows, 128), F32)
        for j in range(taps + 1):
            total = None
            for a in range(devices):
                if j < taps:
                    part = value[a] * delayed(signal, a, j)
                else:
                    part = grad[a] * conv_buf[a, at, :]
                total = part if total is None else total + part
            total = jnp.sum(total, axis=1, keepdims=True) * np.float32(scale)
            sums = jnp.where(lane == j, total, sums)
        small_buf[at, :] = sums

    small_buf[...] = jnp.zeros_like(small_buf)
    over_rows(value_rows)
    gsig_start()
    small_send[...] = small_buf[...].T[:8, :]
    small_start()

    for step in range(groups):
        for up in (True, False):
            @pl.when(sends(step, up))
            def _():
                for h in range(halves):
                    hop(step, h, up).wait_send()

    sig_sent()
    fil_sent()
    resp_sent()
    for _, _, grad_sent in grad_moves:
        grad_sent()
    gfil_sent()
    gsig_sent()
    small_sent()
    gfil_arrive()
    gsig_arrive()
    small_arrive()


def per_device(signal, gate_in, filter_raw, short_kernel, skip_gain, out_weight, cotangent):
    channels, length = signal.shape
    taps = short_kernel.shape[1]
    devices, groups = lax.axis_size("ctx"), lax.axis_size("chan")
    rows = channels // devices
    rows_pad = max(rows, 8)
    halves = 2
    scale = 1.0 / math.sqrt(length * devices)
    twiddle, high, low = tables(devices, length, scale)
    shape = (devices, rows, length)
    tap_table = jnp.concatenate((short_kernel, skip_gain[:, None]), axis=1)
    tap_table = tap_table.reshape(devices, rows, taps + 1)
    out_rows = cotangent.shape[0]
    spec_shape = (devices + 1, rows_pad, 2 * length)
    dims = (devices, groups, rows, rows_pad, length, taps, halves, scale)
    moves = GRAD + halves

    def vmem(*size, dtype=F32):
        return pltpu.VMEM(size, dtype)

    in_vmem, anywhere = pl.BlockSpec(memory_space=pltpu.VMEM), pl.BlockSpec(memory_space=pl.ANY)
    block = jax.ShapeDtypeStruct(shape, F32)
    grad_gate, grad_signal, grad_filter, small = pl.pallas_call(
        functools.partial(kernel, dims),
        out_shape=(block, block, block, jax.ShapeDtypeStruct((devices, 8, 128), F32)),
        in_specs=[anywhere, anywhere, anywhere, in_vmem, anywhere, anywhere, in_vmem, in_vmem, in_vmem],
        out_specs=(in_vmem, anywhere, anywhere, anywhere),
        scratch_shapes=[
            vmem(groups, out_rows, channels),
            vmem(groups, channels, out_rows, dtype=BF16),
            vmem(groups, channels, out_rows, dtype=BF16),
            vmem(groups, out_rows, length),
            vmem(channels, length),
            *[vmem(*shape) for _ in range(10)],
            vmem(128, 128),
            vmem(8, 128),
            *[vmem(*spec_shape) for _ in range(5)],
            pltpu.SemaphoreType.DMA((halves, groups)),
            pltpu.SemaphoreType.DMA((halves, groups)),
            pltpu.SemaphoreType.DMA((halves, groups)),
            pltpu.SemaphoreType.DMA((moves, devices)),
            pltpu.SemaphoreType.DMA((moves, devices)),
            pltpu.SemaphoreType.DMA((moves,)),
            pltpu.SemaphoreType.DMA((3,)),
        ],
        compiler_params=pltpu.CompilerParams(
            collective_id=0, has_side_effects=True, vmem_limit_bytes=56 * 2**20
        ),
    )(
        signal.reshape(shape),
        gate_in.reshape(shape),
        filter_raw.reshape(shape),
        tap_table,
        out_weight.reshape(groups, out_rows, channels),
        cotangent,
        jnp.asarray(twiddle),
        jnp.asarray(high),
        jnp.asarray(low),
    )
    sums = jnp.transpose(small[:, : taps + 1, :rows], (0, 2, 1)).reshape(channels, taps + 1)
    whole = (channels, length)
    return (
        grad_gate.reshape(whole),
        grad_signal.reshape(whole),
        grad_filter.reshape(whole),
        sums[:, :taps],
        sums[:, taps],
    )


def solution(mesh):
    placed = (
        P("chan", "ctx"),
        P("chan", "ctx"),
        P("chan", "ctx"),
        P("chan", None),
        P("chan"),
        P(None, "chan"),
        P("chan", "ctx"),
    )
    return jax.shard_map(
        per_device,
        mesh=mesh,
        in_specs=placed,
        out_specs=(
            P("chan", "ctx"),
            P("chan", "ctx"),
            P("chan", "ctx"),
            P("chan", None),
            P("chan"),
        ),
        check_vma=False,
    )
```

time: 506 us -> 79.1 us (0.16); the launches traced: 497 us -> 78.7 us
  matrix products: 174 us -> 0 us
  waiting for transfers between devices: 159 us -> 0 us
  Pallas kernels: 0 us -> 68.4 us
  local copies, waits for them, and re-layouts: 74.8 us -> 8.79 us
  starting transfers between devices: 36.4 us -> 0 us
  blocking collectives: 22.3 us -> 0 us
  between operations: 15.3 us -> 0.66 us
  other arithmetic: 14.5 us -> 0.84 us
    dot_general x41 -> x0, matrix products: 174 us -> none  [the longest x16 114 us: product_with(): return jnp.einsum('...ac,ab->...bc', operand, table, precision=HIGH)]
    all_to_all x8 -> x0, waiting for transfers between devices: 114 us -> none  [the longest x2 42.2 us: signals(): lax.all_to_all(stacked, 'ctx', split_axis=3, concat_axis=2, tiled=True)]
    pallas_call x0 -> x1, Pallas kernels: none -> 68.4 us  [per_device(): pl.pallas_call(functools.partial(kernel, dims), out_shape=(block, block,...]
    all_gather x1 -> x0, waiting for transfers between devices: 44.4 us -> none  [per_device(): lax.all_gather(cotangent, 'chan', axis=0, tiled=True)]
    another operation x11 -> x0, local copies, waits for them, and re-layouts: 33.6 us -> none  [the longest x4 18.9 us: signals(): stacked = jnp.moveaxis(jnp.stack((real_part, imag_part)), 2, 4)]
    all_to_all x8 -> x0, starting transfers between devices: 32.7 us -> none  [the longest x2 8.94 us: signals(): lax.all_to_all(stacked, 'ctx', split_axis=3, concat_axis=2, tiled=True)]
    psum x1 -> x0, blocking collectives: 22.3 us -> none  [per_device(): skip_sum, kernel_sum = lax.psum((skip_part, kernel_part), 'ctx')]
    slice x11 -> x1, local copies, waits for them, and re-layouts: 13.9 us -> 0.59 us  [per_device(): sums[:, taps]]
  transfers between devices with their start and end apart: 11 -> 0, of which waited for: 7 -> 0; matrix products, arithmetic and copies ran while one was open for 29% -> 0% of each run, Pallas kernels for 0% -> 0%
where the time goes in v1:
time: 79.1 us; the launch traced here: 78.7 us
  Pallas kernels  68.4 us (86%)
  local copies, waits for them, and re-layouts  8.79 us (11%)
  other arithmetic  0.84 us (1%)
    pallas_call x1, Pallas kernels, per_device(): pl.pallas_call(functools.partial(kernel, dims), out_shape=(block, block,...  68.4 us
    unnamed x5, local copies, waits for them, and re-layouts  5.61 us
    concatenate x2, local copies, waits for them, and re-layouts, per_device(): tap_table = jnp.concatenate((short_kernel, skip_gain[:, None]), axis=1)  1.75 us

profile of v1, /device:TPU:0, one launch (start us, length us, event | category | flops | bytes accessed | tf_op | source)
XLA Modules:
  0.0 78.7 jit_solution(5320041142401266262)
XLA Ops:
  0.6 0.9 %copy.29 = f32[512,7]{1,0:T(8,128)S(1)} copy(f32[512,7]{0,1:T(8,128)} %param.13) | data formatting | bytes 28672 | tf_op jit(solution)/shard_map/concatenate | solution.py:487
  1.5 0.9 %concatenate.11 = f32[8,64,1]{2,1,0:T(8,128)S(1)} reshape(f32[512]{0:T(512)} %param.14) | data formatting | bytes 4096 | tf_op jit(solution)/shard_map/concatenate | solution.py:487
  2.4 0.8 %pad_maximum_fusion.taps_ref = f32[8,64,8]{2,1,0:T(8,128)} fusion(f32[8,64,1]{2,1,0:T(8,128)S(1)} %concatenate.11, f32[8,64,7]{2,1,0:T(8,128)S(1)} %bitcast.15), kind=kLoop, calls=%fused_computation | loop fusion | flops 4096 | bytes 32768 | tf_op jit(solution)/shard_map/concatenate | solution.py:487
  3.2 68.4 %shard_map.137 = (f32[8,64,256]{2,1,0:T(8,128)}, f32[8,64,256]{2,1,0:T(8,128)}, f32[8,64,256]{2,1,0:T(8,128)}, f32[8,8,128]{2,1,0:T(8,128)}) custom-call(f32[8,64,256]{2,1,0:T(8,128)} %bitcast.19, f32[8,64,256]{2,1,0:T(8,128)} %bitcast.20, f32[8,64,256]{2,1,0:T(8,128)} %bitcast.21, f32[8,64,8]{2,1,0:T(8,128)} %pad_maximum_fusion.taps_ref, ...), custom_call_target="tpu_custom_call" | custom-call | tf_op jit(solution)/shard_map/pallas_call | solution.py:499
  71.6 0.8 slice_bitcast_fusion
  72.4 0.1 reshape.45
  72.5 0.0 copy-start
  72.5 0.6 slice.13
  73.1 1.9 %copy.33 = f32[512,256]{1,0:T(8,128)} copy(f32[512,256]{1,0:T(8,128)} %bitcast.18) | data formatting | bytes 1048576
  74.9 1.9 %copy.34 = f32[512,256]{1,0:T(8,128)} copy(f32[512,256]{1,0:T(8,128)} %bitcast.17) | data formatting | bytes 1048576
  76.8 1.9 %copy.35 = f32[512,256]{1,0:T(8,128)} copy(f32[512,256]{1,0:T(8,128)} %bitcast.16) | data formatting | bytes 1048576
  78.7 0.0 copy-done
  (1 shorter events, 0.0 us)
Async XLA Ops:
  72.5 6.2 %copy-start = (f32[512,8]{0,1:T(8,128)}, f32[512,8]{0,1:T(8,128)S(1)}, u32[]{:S(2)}) copy-start(f32[512,8]{0,1:T(8,128)S(1)} %reshape.45) | copy-start | bytes 49156

commit v2 on v1

--- a/solution.py
+++ b/solution.py
@@ -12,7 +12,7 @@
 MESH = pl.DeviceIdType.MESH
 F32 = jnp.float32
 BF16 = jnp.bfloat16
-SIG, FIL, RESP, GSIG, GFIL, SMALL, GRAD = range(7)
+SIG, FIL, RESP, SMALL, MOVES = range(5)
 
 
 def split_bf16(value):
@@ -110,20 +110,21 @@
 
 def kernel(
     dims,
-    sig_in, gate_in, fil_in, taps_ref, w_in, cot_in, twiddle, high_ref, low_ref,
+    sig_in, gate_in, fil_in, taps_in, skip_in, w_in, cot_in, twiddle, high_ref, low_ref,
     gate_out, gsig_out, gfil_out, small_out,
     w_buf, wt_hi, wt_lo, cot_all, mix, gate_buf, sig_buf, fil_buf, conv_buf,
-    resp_send, resp_buf, grad_send, grad_buf, gsig_send, gfil_send, small_buf, small_send,
+    resp_send, resp_buf, grad_send, grad_buf, gsig_send, gfil_send, taps_ref, small_buf, small_send, small_land,
     stage, fil_spec, val_spec, grad_spec, work,
     up_sem, down_sem, line_sem, send_sem, recv_sem, local_sem, load_sem,
 ):
-    devices, groups, rows, rows_pad, length, taps, halves, scale = dims
+    devices, groups, rows, length, taps, halves, parts_n, scale = dims
     me, chan = lax.axis_index("ctx"), lax.axis_index("chan")
     half_len = length // halves
     group_rows = min(8, rows)
     row_steps = rows // group_rows
     classes = devices + 1
-    chunk = 3 if classes % 3 == 0 else 1
+    part_rows = rows // parts_n
+    part_steps = row_steps // parts_n
 
     w_copy = pltpu.make_async_copy(w_in, w_buf, load_sem.at[0])
     gate_copy = pltpu.make_async_copy(gate_in, gate_buf, load_sem.at[1])
@@ -237,22 +238,34 @@
     resp_start, resp_arrive, resp_sent = all_to_all(
         RESP, lambda p: resp_send.at[p], lambda p: resp_buf.at[p]
     )
-    gsig_start, gsig_arrive, gsig_sent = all_to_all(
-        GSIG, lambda p: gsig_send.at[p], lambda p: gsig_out.at[p]
+    small_start, small_arrive, small_sent = all_to_all(
+        SMALL, lambda p: small_send, lambda p: small_land.at[p]
     )
-    gfil_start, gfil_arrive, gfil_sent = all_to_all(
-        GFIL, lambda p: gfil_send.at[p], lambda p: gfil_out.at[p]
-    )
-    small_start, small_arrive, small_sent = all_to_all(
-        SMALL, lambda p: small_send, lambda p: small_out.at[p]
-    )
+
+    def part_at(part):
+        return pl.ds(part * part_rows, part_rows)
+
     grad_moves = [
-        all_to_all(
-            GRAD + h,
-            lambda p, h=h: grad_send.at[p, :, lanes(h)],
-            lambda p, h=h: grad_buf.at[p, :, lanes(h)],
-        )
+        [
+            all_to_all(
+                MOVES + h * parts_n + part,
+                lambda p, h=h, part=part: grad_send.at[p, part_at(part), lanes(h)],
+                lambda p, h=h, part=part: grad_buf.at[p, part_at(part), lanes(h)],
+            )
+            for part in range(parts_n)
+        ]
         for h in range(halves)
+    ]
+    back_moves = [
+        [
+            all_to_all(
+                MOVES + (halves + which) * parts_n + part,
+                lambda p, source=source, part=part: source.at[p, part_at(part)],
+                lambda p, target=target, part=part: target.at[p, part_at(part)],
+            )
+            for part in range(parts_n)
+        ]
+        for which, (source, target) in enumerate(((gfil_send, gfil_out), (gsig_send, gsig_out)))
     ]
 
     for h in range(halves):
@@ -260,33 +273,32 @@
     sig_start()
     fil_start()
 
-    def dft(read, target):
-        @pl.loop(0, classes // chunk)
-        def _(i):
-            at = pl.ds(i * chunk, chunk)
-            high, low = split_bf16(read(at))
-            result = jnp.dot(high, low_ref[...], preferred_element_type=F32)
-            result = result + jnp.dot(low, high_ref[...], preferred_element_type=F32)
-            result = result + jnp.dot(high, high_ref[...], preferred_element_type=F32)
-            target[at] = result.reshape(chunk, rows_pad, 2 * length)
+    def dft(read, target, part):
+        span = max(part_rows, 8)
+        at = (slice(None), slice(part * part_rows, part * part_rows + span))
+        high, low = split_bf16(read(at).reshape(classes * span, 2 * length))
+        result = jnp.dot(high, low_ref[...], preferred_element_type=F32)
+        result = result + jnp.dot(low, high_ref[...], preferred_element_type=F32)
+        result = result + jnp.dot(high, high_ref[...], preferred_element_type=F32)
+        target[at] = result.reshape(classes, span, 2 * length)
 
     def plain(at):
-        return stage[at].reshape(chunk * rows_pad, 2 * length)
+        return stage[at]
 
     def product(first, second, conjugate):
         def read(at):
-            a_re, a_im = first[at, :, :length], first[at, :, length:]
-            b_re, b_im = second[at, :, :length], second[at, :, length:]
+            a_re, a_im = first[at][:, :, :length], first[at][:, :, length:]
+            b_re, b_im = second[at][:, :, :length], second[at][:, :, length:]
             if conjugate:
                 real, minus = a_re * b_re + a_im * b_im, a_im * b_re - a_re * b_im
             else:
                 real, minus = a_re * b_re - a_im * b_im, -(a_re * b_im + a_im * b_re)
-            return jnp.concatenate((real, minus), axis=2).reshape(chunk * rows_pad, 2 * length)
+            return jnp.concatenate((real, minus), axis=2)
 
         return read
 
-    def over_rows(body):
-        @pl.loop(0, row_steps)
+    def over_rows(body, part):
+        @pl.loop(part * part_steps, (part + 1) * part_steps)
         def _(r):
             body(pl.ds(pl.multiple_of(r * group_rows, group_rows), group_rows))
 
@@ -324,6 +336,14 @@
         wt_lo[g] = low
 
     cot_copy.wait()
+
+    channels = devices * rows
+    table = jnp.concatenate(
+        (taps_in[...], skip_in[...], jnp.zeros((128 - taps - 1, channels), F32)), axis=0
+    )
+    table = table.T
+    for d in range(devices):
+        taps_ref[d] = table[d * rows : (d + 1) * rows, :]
 
     def mix_add(block, h, first):
         high, low = split_bf16(cot_all[block, :, h * half_len : (h + 1) * half_len])
@@ -356,24 +376,26 @@
             conv.append(total)
         forward_blocks(conv, twiddle, stage_store(at))
 
-    over_rows(conv_rows)
-    dft(plain, val_spec)
+    for part in range(parts_n):
+        over_rows(conv_rows, part)
+        dft(plain, val_spec, part)
 
     for h in range(halves):
         if groups > 1:
             line_arrive(1, h)
 
     fil_arrive()
-    over_rows(
-        lambda at: forward_blocks(
-            [fil_buf[a, at, :] for a in range(devices)], twiddle, stage_store(at)
+    for part in range(parts_n):
+        over_rows(
+            lambda at: forward_blocks(
+                [fil_buf[a, at, :] for a in range(devices)], twiddle, stage_store(at)
+            ),
+            part,
         )
-    )
-    dft(plain, fil_spec)
+        dft(plain, fil_spec, part)
     if groups > 1:
         for h in range(halves):
             mix_step(1, h)
-    dft(product(fil_spec, val_spec, False), work)
 
     def resp_rows(at):
         skip = tap_rows(at)[:, taps : taps + 1]
@@ -381,7 +403,9 @@
         for a in range(devices):
             resp_send[a, at, :] = conv[a] + skip * conv_buf[a, at, :]
 
-    over_rows(resp_rows)
+    for part in range(parts_n):
+        dft(product(fil_spec, val_spec, False), work, part)
+        over_rows(resp_rows, part)
     resp_start()
 
     for step in range(2, groups - 1):
@@ -396,31 +420,17 @@
         here = slice(h * half_len, (h + 1) * half_len)
         for d in range(devices):
             grad_send[d, :, here] = mix[d * rows : (d + 1) * rows, here] * gate_buf[d, :, here]
-        grad_moves[h][0]()
+        for part in range(parts_n):
+            grad_moves[h][part][0]()
 
     resp_arrive()
     for d in range(devices):
         gate_out[d] = mix[d * rows : (d + 1) * rows, :] * resp_buf[d]
-
-    for _, grad_arrive, _ in grad_moves:
-        grad_arrive()
-
-    over_rows(
-        lambda at: forward_blocks(
-            [grad_buf[a, at, :] for a in range(devices)], twiddle, stage_store(at)
-        )
-    )
-    dft(plain, grad_spec)
-    dft(product(val_spec, grad_spec, True), work)
 
     def filter_rows(at):
         parts = inverse_blocks(devices, length, twiddle, lambda q: work[q, at, :])
         for a in range(devices):
             gfil_send[a, at, :] = parts[a]
-
-    over_rows(filter_rows)
-    gfil_start()
-    dft(product(fil_spec, grad_spec, True), work)
 
     def value_rows(at):
         tap = tap_rows(at)
@@ -428,29 +438,43 @@
         value = inverse_blocks(devices, length, twiddle, lambda q: work[q, at, :])
         grad = [grad_buf[a, at, :] for a in range(devices)]
         value = [value[a] + skip * grad[a] for a in range(devices)]
+        sums = [None] * taps
         for a in range(devices):
-            total = tap[:, :1] * value[a]
-            for j in range(1, taps):
-                total = total + tap[:, j : j + 1] * advanced(value, a, j)
+            signal = sig_buf[a, at, :]
+            total = None
+            for j in range(taps):
+                ahead = advanced(value, a, j)
+                term, part_sum = tap[:, j : j + 1] * ahead, ahead * signal
+                total = term if total is None else total + term
+                sums[j] = part_sum if sums[j] is None else sums[j] + part_sum
             gsig_send[a, at, :] = total
-        signal = [sig_buf[a, at, :] for a in range(devices)]
+        skip_sum = grad[0] * conv_buf[0, at, :]
+        for a in range(1, devices):
+            skip_sum = skip_sum + grad[a] * conv_buf[a, at, :]
         lane = lax.broadcasted_iota(jnp.int32, (group_rows, 128), 1)
-        sums = jnp.zeros((group_rows, 128), F32)
-        for j in range(taps + 1):
-            total = None
-            for a in range(devices):
-                if j < taps:
-                    part = value[a] * delayed(signal, a, j)
-                else:
-                    part = grad[a] * conv_buf[a, at, :]
-                total = part if total is None else total + part
-            total = jnp.sum(total, axis=1, keepdims=True) * np.float32(scale)
-            sums = jnp.where(lane == j, total, sums)
-        small_buf[at, :] = sums
+        placed = jnp.zeros((group_rows, 128), F32)
+        for j, each in enumerate(sums + [skip_sum]):
+            total = jnp.sum(each, axis=1, keepdims=True) * np.float32(scale)
+            placed = jnp.where(lane == j, total, placed)
+        small_buf[at, :] = placed
 
     small_buf[...] = jnp.zeros_like(small_buf)
-    over_rows(value_rows)
-    gsig_start()
+    for part in range(parts_n):
+        for h in range(halves):
+            grad_moves[h][part][1]()
+        over_rows(
+            lambda at: forward_blocks(
+                [grad_buf[a, at, :] for a in range(devices)], twiddle, stage_store(at)
+            ),
+            part,
+        )
+        dft(plain, grad_spec, part)
+        dft(product(val_spec, grad_spec, True), work, part)
+        over_rows(filter_rows, part)
+        back_moves[0][part][0]()
+        dft(product(fil_spec, grad_spec, True), work, part)
+        over_rows(value_rows, part)
+        back_moves[1][part][0]()
     small_send[...] = small_buf[...].T[:8, :]
     small_start()
 
@@ -464,14 +488,45 @@
     sig_sent()
     fil_sent()
     resp_sent()
-    for _, _, grad_sent in grad_moves:
-        grad_sent()
-    gfil_sent()
-    gsig_sent()
+    for move in grad_moves + back_moves:
+        for part in range(parts_n):
+            move[part][2]()
     small_sent()
-    gfil_arrive()
-    gsig_arrive()
     small_arrive()
+    per_tile = 128 // rows
+    for tile in range(-(-channels // 128)):
+        total = None
+        for i in range(min(per_tile, devices - tile * per_tile)):
+            each = small_land[tile * per_tile + i]
+            each = each if i == 0 else pltpu.roll(each, i * rows, 1)
+            total = each if total is None else total + each
+        width = min(128, channels - tile * 128)
+        small_out[:, tile * 128 : tile * 128 + width] = total[:, :width]
+    for move in back_moves:
+        for part in range(parts_n):
+            move[part][1]()
+
+
+def handed_on(small_in, *refs):
+    count = (len(refs) - 4) // 2
+    arrays, results = refs[:count], refs[count : 2 * count]
+    taps_out, skip_out, held, sems = refs[2 * count :]
+    loads = [
+        pltpu.make_async_copy(arrays[i], held.at[i], sems.at[0, i]) for i in range(count)
+    ]
+    stores = [
+        pltpu.make_async_copy(held.at[i], results[i], sems.at[1, i]) for i in range(count)
+    ]
+    for load in loads:
+        load.start()
+    taps = taps_out.shape[0]
+    taps_out[...] = small_in[:taps, :]
+    skip_out[...] = small_in[taps : taps + 1, :]
+    for load, store in zip(loads, stores):
+        load.wait()
+        store.start()
+    for store in stores:
+        store.wait()
 
 
 def per_device(signal, gate_in, filter_raw, short_kernel, skip_gain, out_weight, cotangent):
@@ -484,12 +539,11 @@
     scale = 1.0 / math.sqrt(length * devices)
     twiddle, high, low = tables(devices, length, scale)
     shape = (devices, rows, length)
-    tap_table = jnp.concatenate((short_kernel, skip_gain[:, None]), axis=1)
-    tap_table = tap_table.reshape(devices, rows, taps + 1)
     out_rows = cotangent.shape[0]
+    parts_n = 2 if rows % 16 == 0 else 1
     spec_shape = (devices + 1, rows_pad, 2 * length)
-    dims = (devices, groups, rows, rows_pad, length, taps, halves, scale)
-    moves = GRAD + halves
+    dims = (devices, groups, rows, length, taps, halves, parts_n, scale)
+    moves = MOVES + (halves + 2) * parts_n
 
     def vmem(*size, dtype=F32):
         return pltpu.VMEM(size, dtype)
@@ -498,9 +552,9 @@
     block = jax.ShapeDtypeStruct(shape, F32)
     grad_gate, grad_signal, grad_filter, small = pl.pallas_call(
         functools.partial(kernel, dims),
-        out_shape=(block, block, block, jax.ShapeDtypeStruct((devices, 8, 128), F32)),
-        in_specs=[anywhere, anywhere, anywhere, in_vmem, anywhere, anywhere, in_vmem, in_vmem, in_vmem],
-        out_specs=(in_vmem, anywhere, anywhere, anywhere),
+        out_shape=(block, block, block, jax.ShapeDtypeStruct((8, channels), F32)),
+        in_specs=[anywhere, anywhere, anywhere, in_vmem, in_vmem, anywhere, anywhere, in_vmem, in_vmem, in_vmem],
+        out_specs=(in_vmem, anywhere, anywhere, in_vmem),
         scratch_shapes=[
             vmem(groups, out_rows, channels),
             vmem(groups, channels, out_rows, dtype=BF16),
@@ -508,8 +562,10 @@
             vmem(groups, out_rows, length),
             vmem(channels, length),
             *[vmem(*shape) for _ in range(10)],
+            vmem(devices, rows, 128),
             vmem(128, 128),
             vmem(8, 128),
+            vmem(devices, 8, 128),
             *[vmem(*spec_shape) for _ in range(5)],
             pltpu.SemaphoreType.DMA((halves, groups)),
             pltpu.SemaphoreType.DMA((halves, groups)),
@@ -526,21 +582,32 @@
         signal.reshape(shape),
         gate_in.reshape(shape),
         filter_raw.reshape(shape),
-        tap_table,
+        short_kernel.T,
+        skip_gain[None, :],
         out_weight.reshape(groups, out_rows, channels),
         cotangent,
         jnp.asarray(twiddle),
         jnp.asarray(high),
         jnp.asarray(low),
     )
-    sums = jnp.transpose(small[:, : taps + 1, :rows], (0, 2, 1)).reshape(channels, taps + 1)
+    grad_gate, grad_signal, grad_filter, grad_kernel, grad_skip = pl.pallas_call(
+        handed_on,
+        out_shape=(block,) * 3
+        + (
+            jax.ShapeDtypeStruct((taps, channels), F32),
+            jax.ShapeDtypeStruct((1, channels), F32),
+        ),
+        in_specs=[in_vmem] + [anywhere] * 3,
+        out_specs=(anywhere,) * 3 + (in_vmem,) * 2,
+        scratch_shapes=[vmem(3, *shape), pltpu.SemaphoreType.DMA((2, 3))],
+    )(small, grad_gate, grad_signal, grad_filter)
     whole = (channels, length)
     return (
         grad_gate.reshape(whole),
         grad_signal.reshape(whole),
         grad_filter.reshape(whole),
-        sums[:, :taps],
-        sums[:, taps],
+        grad_kernel.T,
+        grad_skip[0],
     )
 
 

time: 79.1 us -> 69.5 us (0.88)
  local copies, waits for them, and re-layouts: 8.79 us -> 0 us
  other arithmetic: 0.84 us -> 0 us
    unnamed x5 -> x0, local copies, waits for them, and re-layouts: 5.61 us -> none
    pallas_call x0 -> x1, Pallas kernels: none -> 3.56 us  [per_device(): pl.pallas_call(handed_on, out_shape=(block,) * 3 + (jax.ShapeDtypeStruct(...]
    pallas_call x1, Pallas kernels: 68.4 us -> 64.9 us  [per_device(): pl.pallas_call(functools.partial(kernel, dims), out_shape=(block, block,...]
    concatenate x2 -> x0, local copies, waits for them, and re-layouts: 1.75 us -> none  [per_device(): tap_table = jnp.concatenate((short_kernel, skip_gain[:, None]), axis=1)]
    concatenate x1 -> x0, other arithmetic: 0.84 us -> none  [per_device(): tap_table = jnp.concatenate((short_kernel, skip_gain[:, None]), axis=1)]
where the time goes in v2:
time: 69.5 us; the launch traced here: 69.3 us
  Pallas kernels  68.5 us (99%)
  between operations  0.8 us (1%)
    pallas_call x1, Pallas kernels, per_device(): pl.pallas_call(functools.partial(kernel, dims), out_shape=(block, block,...  64.9 us
    pallas_call x1, Pallas kernels, per_device(): pl.pallas_call(handed_on, out_shape=(block,) * 3 + (jax.ShapeDtypeStruct(...  3.56 us

profile of v2, /device:TPU:0, one launch (start us, length us, event | category | flops | bytes accessed | tf_op | source)
XLA Modules:
  0.0 69.3 jit_solution(7532415028811869367)
XLA Ops:
  0.6 64.9 %shard_map.137 = (f32[8,64,256]{2,1,0:T(8,128)}, f32[8,64,256]{2,1,0:T(8,128)}, f32[8,64,256]{2,1,0:T(8,128)}, f32[8,512]{1,0:T(8,128)}) custom-call(f32[8,64,256]{2,1,0:T(8,128)} %bitcast.12, f32[8,64,256]{2,1,0:T(8,128)} %bitcast.13, f32[8,64,256]{2,1,0:T(8,128)} %bitcast.14, f32[7,512]{1,0:T(8,128)} %bitcast.15, f32[1,512]{1,0:T(1,128)} %bitcast.16, ...), custom_call_target="tpu_custom_call" | custom-call | tf_op jit(solution)/shard_map/pallas_call | solution.py:553
  65.6 3.6 %shard_map.138 = (f32[8,64,256]{2,1,0:T(8,128)}, f32[8,64,256]{2,1,0:T(8,128)}, f32[8,64,256]{2,1,0:T(8,128)}, f32[7,512]{1,0:T(8,128)}, f32[1,512]{1,0:T(1,128)}) custom-call(f32[8,512]{1,0:T(8,128)} %get-tuple-element.14.small_in, f32[8,64,256]{2,1,0:T(8,128)} %get-tuple-element.15.refs_0_, f32[8,64,256]{2,1,0:T(8,128)} %get-tuple-element.16.refs_1_, ...), custom_call_target="tpu_custom_call" | custom-call | tf_op jit(solution)/shard_map/pallas_call | solution.py:593

commit v3 on v2

--- a/solution.py
+++ b/solution.py
@@ -511,11 +511,16 @@
     count = (len(refs) - 4) // 2
     arrays, results = refs[:count], refs[count : 2 * count]
     taps_out, skip_out, held, sems = refs[2 * count :]
+    cuts = sems.shape[2]
+    span = held.shape[1] // cuts
+    pieces = [(i, k, pl.ds(k * span, span)) for k in range(cuts) for i in range(count)]
     loads = [
-        pltpu.make_async_copy(arrays[i], held.at[i], sems.at[0, i]) for i in range(count)
+        pltpu.make_async_copy(arrays[i].at[at], held.at[i, at], sems.at[0, i, k])
+        for i, k, at in pieces
     ]
     stores = [
-        pltpu.make_async_copy(held.at[i], results[i], sems.at[1, i]) for i in range(count)
+        pltpu.make_async_copy(held.at[i, at], results[i].at[at], sems.at[1, i, k])
+        for i, k, at in pieces
     ]
     for load in loads:
         load.start()
@@ -599,7 +604,7 @@
         ),
         in_specs=[in_vmem] + [anywhere] * 3,
         out_specs=(anywhere,) * 3 + (in_vmem,) * 2,
-        scratch_shapes=[vmem(3, *shape), pltpu.SemaphoreType.DMA((2, 3))],
+        scratch_shapes=[vmem(3, *shape), pltpu.SemaphoreType.DMA((2, 3, 4))],
     )(small, grad_gate, grad_signal, grad_filter)
     whole = (channels, length)
     return (

time: 69.5 us -> 69.6 us (level)
  no operation moved by 1% of the time
where the time goes in v3:
time: 69.6 us; the launch traced here: 69.4 us
  Pallas kernels  68.6 us (99%)
  between operations  0.8 us (1%)
    pallas_call x1, Pallas kernels, per_device(): pl.pallas_call(functools.partial(kernel, dims), out_shape=(block, block,...  64.9 us
    pallas_call x1, Pallas kernels, per_device(): pl.pallas_call(handed_on, out_shape=(block,) * 3 + (jax.ShapeDtypeStruct(...  3.65 us

profile of v3, /device:TPU:0, one launch (start us, length us, event | category | flops | bytes accessed | tf_op | source)
XLA Modules:
  0.0 69.4 jit_solution(7967919787052143286)
XLA Ops:
  0.6 64.9 %shard_map.137 = (f32[8,64,256]{2,1,0:T(8,128)}, f32[8,64,256]{2,1,0:T(8,128)}, f32[8,64,256]{2,1,0:T(8,128)}, f32[8,512]{1,0:T(8,128)}) custom-call(f32[8,64,256]{2,1,0:T(8,128)} %bitcast.12, f32[8,64,256]{2,1,0:T(8,128)} %bitcast.13, f32[8,64,256]{2,1,0:T(8,128)} %bitcast.14, f32[7,512]{1,0:T(8,128)} %bitcast.15, f32[1,512]{1,0:T(1,128)} %bitcast.16, ...), custom_call_target="tpu_custom_call" | custom-call | tf_op jit(solution)/shard_map/pallas_call | solution.py:558
  65.6 3.7 %shard_map.138 = (f32[8,64,256]{2,1,0:T(8,128)}, f32[8,64,256]{2,1,0:T(8,128)}, f32[8,64,256]{2,1,0:T(8,128)}, f32[7,512]{1,0:T(8,128)}, f32[1,512]{1,0:T(1,128)}) custom-call(f32[8,512]{1,0:T(8,128)} %get-tuple-element.14.small_in, f32[8,64,256]{2,1,0:T(8,128)} %get-tuple-element.15.refs_0_, f32[8,64,256]{2,1,0:T(8,128)} %get-tuple-element.16.refs_1_, ...), custom_call_target="tpu_custom_call" | custom-call | tf_op jit(solution)/shard_map/pallas_call | solution.py:598
